TPU v7x, 512 devices: a whole 4x4x16 slice. The times are simulated.
512 devices in a mesh: seq: 64 (over z, x_lo, core), fsdp: 8 (over y, x_hi).
Axes of the slice: x: 4 (x_hi: 2, x_lo: 2; x = x_hi * 2 + x_lo), y: 4, z: 16, core: 2. Of those that a mesh axis runs over, the one named last changes fastest.
Arguments:
- q_s: bfloat16 [8, 64, 128, 1536], P('fsdp', 'seq'), may hold values from -48 to 48, as said below
- k_s: bfloat16 [8, 64, 128, 1536], P('fsdp', 'seq'), may hold values from -6 to 6, as said below
- v_s: bfloat16 [8, 64, 128, 1536], P('fsdp', 'seq'), may hold values from -6 to 6
- time_index: int32 [8], P('fsdp'), may hold values from 0 to 63
- ada_table: float32 [64, 2, 1536], replicated, may hold values from -3 to 3
- w_temporal: bfloat16 [1536, 4608], P('seq', 'fsdp'), may hold values from -0.15625 to 0.15625
Outputs:
- temporal_out: bfloat16 [8, 64, 128, 1536], P('fsdp', 'seq')
Inputs may be any that keep to these rules, and one draw needn't show every extreme that they name: `q_s`: real-valued entries. `k_s`: real-valued entries.
All inputs are finite; a program needn't handle non-finite values.
Results may differ from a plain program's by a relative error of at most 0.015.
Values may be sent and summed in bfloat16 or wider, within the bound.
No kernel may reach another device: no remote copies, remote signals or barrier semaphores. Data moves between devices by JAX's collectives and lax.ppermute only.
A program may use at most 64 MiB of HBM per device.

v0:
```python
import jax
import jax.numpy as jnp
from jax import lax
from jax.sharding import PartitionSpec as P

HEADS = 12
HEAD_SIZE = 128
ITERS = 3
relax_power = 0.8
norm_eps = 1e-06


def balanced_transport(logit_scores):
    potential_col = jnp.zeros_like(logit_scores[..., :1, :])
    potential_row = jnp.zeros_like(logit_scores[..., :, :1])
    for turn in range(ITERS):
        potential_row = -relax_power * jax.nn.logsumexp(
            logit_scores + potential_col, axis=-1, keepdims=True
        )
        potential_col = -relax_power * jax.nn.logsumexp(
            logit_scores + potential_row, axis=-2, keepdims=True
        )
    return jnp.exp(logit_scores + potential_row + potential_col).astype(jnp.bfloat16)


def temporal_attend(triple, logit_scale):
    temporal_logits = (
        jnp.einsum(
            "vfphd,vgphd->vphfg",
            triple[:, :, :, 0],
            triple[:, :, :, 1],
            preferred_element_type=jnp.float32,
        )
        * logit_scale
    )
    temporal_transport = balanced_transport(temporal_logits)
    temporal = jnp.einsum(
        "vphfg,vgphd->vfphd",
        temporal_transport,
        triple[:, :, :, 2],
        preferred_element_type=jnp.float32,
    )
    return temporal.astype(jnp.bfloat16)


def project(tokens, w_temporal):
    gathered = lax.all_gather(w_temporal, "fsdp", axis=1, tiled=True)
    whole = lax.all_gather(gathered, "seq", axis=0, tiled=True)
    return jnp.dot(tokens, whole, preferred_element_type=jnp.float32).astype(jnp.bfloat16)


def local(q_s, k_s, v_s, time_index, ada_table, w_temporal):
    positions = q_s.shape[2]
    width = HEADS * HEAD_SIZE
    logit_scale = 1.0 / HEAD_SIZE**0.5
    query_rows = q_s[0, 0].reshape(positions, HEADS, HEAD_SIZE)
    key_rows = k_s[0, 0].reshape(positions, HEADS, HEAD_SIZE)
    value_rows = v_s[0, 0].reshape(positions, HEADS, HEAD_SIZE)
    logit_scores = (
        jnp.einsum("pgl,bgl->gpb", query_rows, key_rows, preferred_element_type=jnp.float32)
        * logit_scale
    )
    transport_plan = balanced_transport(logit_scores)
    spatial_result = jnp.einsum(
        "bzg,gbq->zbq", transport_plan, value_rows, preferred_element_type=jnp.float32
    )
    spatial_result = spatial_result.reshape(positions, width).astype(jnp.bfloat16)
    selector = (jnp.arange(ada_table.shape[0]) == time_index[0]).astype(jnp.float32)
    modulate = jnp.einsum("t,tcw->cw", selector, ada_table, precision=lax.Precision.HIGHEST)
    hidden = spatial_result.astype(jnp.float32)
    scaled = hidden * lax.rsqrt(jnp.mean(hidden * hidden, axis=-1, keepdims=True) + norm_eps)
    modulated = (scaled * (1.0 + modulate[0]) + modulate[1]).astype(jnp.bfloat16)
    relayed = lax.all_to_all(modulated[None], "seq", split_axis=1, concat_axis=0, tiled=True)
    frames, local_pos = (relayed.shape[0], relayed.shape[1])
    triple = project(relayed.reshape(frames * local_pos, width), w_temporal)
    triple = triple.reshape(1, frames, local_pos, 3, HEADS, HEAD_SIZE)
    temporal = temporal_attend(triple, logit_scale).reshape(frames, local_pos, width)
    returned = lax.all_to_all(temporal, "seq", split_axis=0, concat_axis=1, tiled=True)
    return returned[None]


def solution(mesh):
    in_specs = (
        P("fsdp", "seq", None, None),
        P("fsdp", "seq", None, None),
        P("fsdp", "seq", None, None),
        P("fsdp"),
        P(),
        P("seq", "fsdp"),
    )
    out_specs = P("fsdp", "seq", None, None)
    return jax.shard_map(local, mesh=mesh, in_specs=in_specs, out_specs=out_specs, check_vma=False)
```

profile of v0, /device:TPU:1, one launch (start us, length us, event | category | flops | bytes accessed | tf_op | source)
XLA Modules:
  0.0 256.5 jit_solution(9671927672942869763)
XLA Ops:
  6.5 30.9 %all-gather = bf16[8,576,24]{1,2,0:T(8,128)(2,1)S(1)} all-gather(bf16[1,576,24]{1,2,0:T(8,128)(2,1)} %bitcast.56), channel_id=1, replica_groups=mesh['seq'=64,'fsdp'=8] {'fsdp'}, dimensions={0}, use_global_device_ids=true | all-gather | bytes 248832 | tf_op jit(solution)/shard_map/all_gather | solution.py:47
  37.5 0.9 reshape.479
  38.4 1.2 copy.71
  40.1 0.5 fusion.16
  40.6 0.5 exponential_reduce_fusion.11
  42.1 0.5 exponential_reduce_fusion.9
  43.5 0.5 exponential_reduce_fusion.7
  44.7 0.5 multiply_reduce_fusion
  46.1 0.4 fusion.2
  46.7 0.6 copy.113
  47.3 0.5 broadcast.318
  47.9 3.0 %reduce.30 = bf16[128,1536]{1,0:T(8,128)(2,1)S(1)} reduce(bf16[128,1,1536]{2,1,0:T(2,128)(2,1)S(1)} %bitcast.49, bf16[]{:T(256)} %broadcast.318), dimensions={1}, to_apply=%bitcast.46.reduce_sub_computation | reduce | bytes 786434
  51.0 54.3 %all_to_all.8 = bf16[64,2,1536]{2,1,0:T(2,128)(2,1)S(1)} all-to-all(bf16[64,2,1536]{2,1,0:T(2,128)(2,1)S(1)} %reshape.485), channel_id=1, replica_groups=mesh['seq'=64,'fsdp'=8] {'seq'}, dimensions={0} | all-to-all | bytes 786432 | tf_op jit(solution)/shard_map/all_to_all | solution.py:73
  105.3 0.3 reshape.486
  105.7 93.0 %all-gather.3.cloned.1.call-done = bf16[1536,4608]{1,0:T(8,128)(2,1)} async-done(((bf16[24,4608]{1,0:T(8,128)(2,1)}), bf16[1536,4608]{1,0:T(8,128)(2,1)}) %all-gather.3.cloned.1.call-update) | async-done | bytes 14155792 | tf_op jit(solution)/shard_map/all_gather | solution.py:48
  198.7 7.0 %convolution_convert_fusion = bf16[128,4608]{1,0:T(8,128)(2,1)S(1)} fusion(bf16[1536,4608]{1,0:T(8,128)(2,1)} %all-gather.3.cloned.1.call-done, bf16[1,128,1536]{2,0,1:T(2,128)(2,1)S(1)} %bitcast.50), kind=kOutput, calls=%fused_computation | convolution fusion | flops 1812529152 | bytes 15728640 | tf_op jit(solution)/shard_map/dot_general | solution.py:49
  205.7 0.9 reshape.472
  206.9 0.5 fusion.17
  207.3 0.5 exponential_reduce_fusion.5
  208.8 0.5 exponential_reduce_fusion.3
  210.3 0.5 exponential_reduce_fusion.1
  211.5 0.4 fusion.1
  212.4 36.4 %all_to_all.9 = bf16[64,2,1536]{2,1,0:T(2,128)(2,1)S(1)} all-to-all(bf16[64,2,1536]{2,1,0:T(2,128)(2,1)S(1)} %reshape.482), channel_id=1, replica_groups=mesh['seq'=64,'fsdp'=8] {'seq'}, dimensions={0} | all-to-all | bytes 786432 | tf_op jit(solution)/shard_map/all_to_all | solution.py:78
  248.8 0.9 broadcast_in_dim.2
  (60 shorter events, 6.6 us)
Async XLA Ops:
  6.5 39.5 %copy-start = (f32[64,2,1536]{2,1,0:T(2,128)S(1)}, f32[64,2,1536]{2,1,0:T(2,128)}, u32[]{:S(2)}) copy-start(f32[64,2,1536]{2,1,0:T(2,128)} %param.10) | copy-start | bytes 2359300
  6.5 33.1 %copy-start.1 = (bf16[1,1,128,1536]{3,2,1,0:T(8,128)(2,1)S(1)}, bf16[1,1,128,1536]{3,2,1,0:T(8,128)(2,1)}, u32[]{:S(2)}) copy-start(bf16[1,1,128,1536]{3,2,1,0:T(8,128)(2,1)} %param.7) | copy-start | bytes 1179652
  6.5 33.3 %copy-start.2 = (bf16[1,1,128,1536]{3,2,1,0:T(8,128)(2,1)S(1)}, bf16[1,1,128,1536]{3,2,1,0:T(8,128)(2,1)}, u32[]{:S(2)}) copy-start(bf16[1,1,128,1536]{3,2,1,0:T(8,128)(2,1)} %param.8) | copy-start | bytes 1179652
  6.5 192.1 %all-gather.3.cloned.1.call-start = ((), (), s32[]{:S(2)}) async-start(), calls=%async_computation.2 | async-start | bytes 14376960 | tf_op jit(solution)/shard_map/all_gather | solution.py:48
Sparse Core Ops, SparseCore 0:
  38.5 160.0 all-gather.2
where the time goes:
time: 257 us
  blocking collectives  122 us (47%)
  waiting for transfers between devices  93 us (36%)
  between operations  14.5 us (6%)
  other arithmetic  11 us (4%)
  matrix products  9.32 us (4%)
  local copies, waits for them, and re-layouts  6.94 us (3%)
    all_gather x1, waiting for transfers between devices, project(): whole = lax.all_gather(gathered, 'seq', axis=0, tiled=True)  93 us
    all_to_all x1, blocking collectives, local(): lax.all_to_all(modulated[None], 'seq', split_axis=1, concat_axis=0, tiled...  54.3 us
    all_to_all x1, blocking collectives, local(): lax.all_to_all(temporal, 'seq', split_axis=0, concat_axis=1, tiled=True)  36.4 us
    all_gather x1, blocking collectives, project(): gathered = lax.all_gather(w_temporal, 'fsdp', axis=1, tiled=True)  30.9 us
    dot_general x1, matrix products, project(): jnp.dot(tokens, whole, preferred_element_type=jnp.float32)  7.04 us
  transfers between devices with their start and end apart: 1, of which 1 were waited for; matrix products, arithmetic and copies ran while one was open for 5% of the time, Pallas kernels for 0%

commit v1 on v0

--- a/solution.py
+++ b/solution.py
@@ -8,6 +8,11 @@
 ITERS = 3
 relax_power = 0.8
 norm_eps = 1e-06
+
+
+def exchange_gather(shard, mesh_axis, dim):
+    repeated = jnp.stack([shard] * lax.axis_size(mesh_axis))
+    return jnp.concatenate(lax.all_to_all(repeated, mesh_axis, 0, 0), axis=dim)
 
 
 def balanced_transport(logit_scores):
@@ -45,7 +50,7 @@
 
 def project(tokens, w_temporal):
     gathered = lax.all_gather(w_temporal, "fsdp", axis=1, tiled=True)
-    whole = lax.all_gather(gathered, "seq", axis=0, tiled=True)
+    whole = exchange_gather(gathered, "seq", 0)
     return jnp.dot(tokens, whole, preferred_element_type=jnp.float32).astype(jnp.bfloat16)
 
 

time: 257 us -> 753 us (2.93)
  waiting for transfers between devices: 93 us -> 608 us
  blocking collectives: 122 us -> 72 us
  starting transfers between devices: 0.01 us -> 36 us
  between operations: 14.5 us -> 1.17 us
  local copies, waits for them, and re-layouts: 6.94 us -> 15.1 us
    all_to_all x0 -> x2, waiting for transfers between devices: none -> 608 us  [the longest x1 608 us: exchange_gather(): return jnp.concatenate(lax.all_to_all(repeated, mesh_axis, 0, 0), axis=dim)]
    all_gather x1 -> x0, waiting for transfers between devices: 93 us -> none  [project(): whole = lax.all_gather(gathered, 'seq', axis=0, tiled=True)]
    all_to_all x1 -> x0, blocking collectives: 54.3 us -> none  [local(): lax.all_to_all(modulated[None], 'seq', split_axis=1, concat_axis=0, tiled...]
    all_to_all x0 -> x2, starting transfers between devices: none -> 36 us  [the longest x1 18.1 us: local(): lax.all_to_all(modulated[None], 'seq', split_axis=1, concat_axis=0, tiled...]
  transfers between devices with their start and end apart: 1 -> 2, of which waited for: 1 -> 1; matrix products, arithmetic and copies ran while one was open for 5% -> 0% of each run, Pallas kernels for 0% -> 0%
where the time goes in v1:
time: 753 us
  waiting for transfers between devices  608 us (81%)
  blocking collectives  72 us (10%)
  starting transfers between devices  36 us (5%)
  local copies, waits for them, and re-layouts  15.1 us (2%)
  other arithmetic  11.1 us (1%)
  matrix products  9.32 us (1%)
    all_to_all x1, waiting for transfers between devices, exchange_gather(): return jnp.concatenate(lax.all_to_all(repeated, mesh_axis, 0, 0), axis=dim)  608 us
    all_to_all x1, blocking collectives, local(): lax.all_to_all(temporal, 'seq', split_axis=0, concat_axis=1, tiled=True)  41 us
    all_gather x1, blocking collectives, project(): gathered = lax.all_gather(w_temporal, 'fsdp', axis=1, tiled=True)  31 us
    all_to_all x1, starting transfers between devices, local(): lax.all_to_all(modulated[None], 'seq', split_axis=1, concat_axis=0, tiled...  18.1 us
    all_to_all x1, starting transfers between devices, exchange_gather(): return jnp.concatenate(lax.all_to_all(repeated, mesh_axis, 0, 0), axis=dim)  17.9 us
  transfers between devices with their start and end apart: 2, of which 1 were waited for; matrix products, arithmetic and copies ran while one was open for 0% of the time, Pallas kernels for 0%

profile of v1, /device:TPU:1, one launch (start us, length us, event | category | flops | bytes accessed | tf_op | source)
XLA Modules:
  0.0 752.6 jit_solution(17460975694439020911)
XLA Ops:
  0.0 1.3 copy.76
  1.3 1.2 copy.72
  2.5 1.2 copy.73
  3.7 0.5 fusion.16
  4.2 0.5 exponential_reduce_fusion.11
  5.7 0.5 exponential_reduce_fusion.9
  7.1 0.5 exponential_reduce_fusion.7
  8.3 0.5 multiply_reduce_fusion
  10.4 0.6 copy.114
  11.0 0.5 broadcast.320
  11.5 3.0 reduce.30
  14.5 0.9 reshape.491
  15.4 18.1 %all-to-all-start = ((bf16[64,2,1536]{2,1,0:T(2,128)(2,1)}), bf16[64,2,1536]{2,1,0:T(2,128)(2,1)S(1)}, u32[]{:S(2)}, u32[]{:S(2)}) async-start(bf16[64,2,1536]{2,1,0:T(2,128)(2,1)} %reshape.491), calls=%async_computation | async-start | bytes 786432 | tf_op jit(solution)/shard_map/all_to_all | solution.py:78
  33.5 31.0 %all-gather = bf16[8,576,24]{1,2,0:T(8,128)(2,1)S(1)} all-gather(bf16[1,576,24]{1,2,0:T(8,128)(2,1)S(1)} %bitcast.57), channel_id=1, replica_groups=mesh['seq'=64,'fsdp'=8] {'fsdp'}, dimensions={0}, use_global_device_ids=true | all-gather | bytes 248832 | tf_op jit(solution)/shard_map/all_gather | solution.py:52
  64.7 6.0 stack.2
  70.8 17.9 %all-to-all-start.1 = ((bf16[64,24,4608]{2,1,0:T(8,128)(2,1)}), bf16[64,24,4608]{2,1,0:T(8,128)(2,1)}, u32[]{:S(2)}, u32[]{:S(2)}) async-start(bf16[64,24,4608]{2,1,0:T(8,128)(2,1)} %stack.2), calls=%async_computation.1 | async-start | bytes 28311552 | tf_op jit(solution)/shard_map/all_to_all | solution.py:15
  89.0 607.9 %all-to-all-done.1 = bf16[64,24,4608]{2,1,0:T(8,128)(2,1)} async-done(((bf16[64,24,4608]{2,1,0:T(8,128)(2,1)}), bf16[64,24,4608]{2,1,0:T(8,128)(2,1)}, u32[]{:S(2)}, u32[]{:S(2)}) %all-to-all-start.1) | async-done | bytes 14155808 | tf_op jit(solution)/shard_map/all_to_all | solution.py:15
  697.0 7.0 convolution_convert_fusion
  704.0 0.9 reshape.478
  705.6 0.5 exponential_reduce_fusion.5
  707.1 0.5 exponential_reduce_fusion.3
  708.6 0.5 exponential_reduce_fusion.1
  710.7 41.0 %all_to_all.23 = bf16[64,2,1536]{2,1,0:T(2,128)(2,1)S(1)} all-to-all(bf16[64,2,1536]{2,1,0:T(2,128)(2,1)S(1)} %reshape.488), channel_id=1, replica_groups=mesh['seq'=64,'fsdp'=8] {'seq'}, dimensions={0} | all-to-all | bytes 786432 | tf_op jit(solution)/shard_map/all_to_all | solution.py:83
  751.7 0.9 broadcast_in_dim.2
  (59 shorter events, 7.8 us)
Async XLA Ops:
  0.0 9.7 %copy-start = (f32[64,2,1536]{2,1,0:T(2,128)S(1)}, f32[64,2,1536]{2,1,0:T(2,128)}, u32[]{:S(2)}) copy-start(f32[64,2,1536]{2,1,0:T(2,128)} %param.10) | copy-start | bytes 2359300
  0.0 33.5 %copy-start.1 = (bf16[24,576]{1,0:T(8,128)(2,1)S(1)}, bf16[24,576]{1,0:T(8,128)(2,1)}, u32[]{:S(2)}) copy-start(bf16[24,576]{1,0:T(8,128)(2,1)} %param.11) | copy-start | bytes 82948
  15.4 49.3 %all-to-all-start = ((bf16[64,2,1536]{2,1,0:T(2,128)(2,1)}), bf16[64,2,1536]{2,1,0:T(2,128)(2,1)S(1)}, u32[]{:S(2)}, u32[]{:S(2)}) async-start(bf16[64,2,1536]{2,1,0:T(2,128)(2,1)} %reshape.491), calls=%async_computation | async-start | bytes 786432 | tf_op jit(solution)/shard_map/all_to_all | solution.py:78
  70.8 626.2 %all-to-all-start.1 = ((bf16[64,24,4608]{2,1,0:T(8,128)(2,1)}), bf16[64,24,4608]{2,1,0:T(8,128)(2,1)}, u32[]{:S(2)}, u32[]{:S(2)}) async-start(bf16[64,24,4608]{2,1,0:T(8,128)(2,1)} %stack.2), calls=%async_computation.1 | async-start | bytes 28311552 | tf_op jit(solution)/shard_map/all_to_all | solution.py:15
